TPU v7x, 256 devices: a whole 4x4x8 slice. The times are simulated.
256 devices in a mesh: dp: 32 (over z, x), tensor: 8 (over y, core).
Axes of the slice: x: 4, y: 4, z: 8, core: 2. Of those that a mesh axis runs over, the one named last changes fastest.
Arguments:
- tokens: bfloat16 [65536, 8192], P('dp', 'tensor'), may hold values from -6 to 6
- base_value_weight: bfloat16 [8192, 1024], P('tensor'), may hold values from -0.0625 to 0.0625
- adapter_down_weight: bfloat16 [512, 8192, 64], P('dp', 'tensor'), may hold values from -0.0625 to 0.0625
- adapter_up_weight: bfloat16 [512, 64, 1024], P('dp', None, 'tensor'), may hold values from -0.75 to 0.75
- request_adapter_index: int32 [128], P('dp'), may hold values from 0 to 511
- storage_index_table: int32 [512], replicated, may hold values from 0 to 511, each once
Outputs:
- values_out: bfloat16 [65536, 1024], P('dp', 'tensor')
Inputs may be any that keep to these rules, and one draw needn't show every extreme that they name: `request_adapter_index`: each adapter id names an adapter. storage_index_table is a permutation of the storage positions.
All inputs are finite; a program needn't handle non-finite values.
Results may differ from a plain program's by a relative error of at most 0.003.
Values may be sent and summed in bfloat16 or wider, within the bound.
A program may use at most 128 MiB of HBM per device.

v0:
```python
import jax
import jax.numpy as jnp
from jax import lax
from jax.sharding import PartitionSpec as P

adapter_scale = 0.5


def shards(
    tokens,
    base_value_weight,
    adapter_down_weight,
    adapter_up_weight,
    request_adapter_index,
    storage_index_table,
):
    n_rows, width = tokens.shape
    requests_here = request_adapter_index.shape[0]
    seq_len = n_rows // requests_here
    owned_columns = adapter_down_weight.shape[0]
    adapter_rank_size = adapter_down_weight.shape[2]
    local_columns = adapter_up_weight.shape[2]
    all_adapters = storage_index_table.shape[0]
    down_width = width * adapter_rank_size
    base_projection = lax.psum_scatter(
        lax.dot_general(
            base_value_weight, tokens, (((0,), (1,)), ((), ())), preferred_element_type=jnp.float32
        ),
        "tensor",
        scatter_dimension=0,
        tiled=True,
    ).T
    every_id = lax.all_gather(request_adapter_index, "dp", axis=0, tiled=True)
    catalog = lax.broadcasted_iota(jnp.int32, (every_id.shape[0], all_adapters), 1)
    picked = (every_id[:, None] == catalog).astype(jnp.int32)
    positions = jnp.sum(picked * storage_index_table[None, :], axis=1)
    local_place = positions - lax.axis_index("dp") * owned_columns
    owner_slots = lax.broadcasted_iota(jnp.int32, (every_id.shape[0], owned_columns), 1)
    match = (local_place[:, None] == owner_slots).astype(jnp.bfloat16)
    panels = jnp.concatenate(
        (
            adapter_down_weight.reshape(owned_columns, down_width),
            adapter_up_weight.reshape(owned_columns, adapter_rank_size * local_columns),
        ),
        axis=1,
    )
    outgoing = jnp.dot(match, panels, preferred_element_type=jnp.bfloat16)
    outgoing = outgoing.reshape(lax.axis_size("dp"), requests_here, panels.shape[1])
    fetched = jnp.sum(
        lax.all_to_all(outgoing, "dp", split_axis=0, concat_axis=0, tiled=True), axis=0
    )
    down_sel = fetched[:, :down_width].reshape(requests_here, width, adapter_rank_size)
    up_sel = fetched[:, down_width:].reshape(requests_here, adapter_rank_size, local_columns)
    grouped = tokens.reshape(requests_here, seq_len, width)
    low_part = jnp.einsum("rsd,rdk->rsk", grouped, down_sel, preferred_element_type=jnp.float32)
    low = lax.psum(low_part, "tensor").astype(jnp.bfloat16)
    adapter_update = jnp.einsum("rsk,rkc->rsc", low, up_sel, preferred_element_type=jnp.float32)
    adapter_update = adapter_update.reshape(n_rows, local_columns)
    return (base_projection + adapter_scale * adapter_update).astype(jnp.bfloat16)


def solution(mesh):
    return jax.shard_map(
        shards,
        mesh=mesh,
        in_specs=(
            P("dp", "tensor"),
            P("tensor", None),
            P("dp", "tensor", None),
            P("dp", None, "tensor"),
            P("dp"),
            P(),
        ),
        out_specs=P("dp", "tensor"),
        check_vma=False,
    )
```

profile of v0, /device:TPU:102, one launch (start us, length us, event | category | flops | bytes accessed | tf_op | source)
XLA Modules:
  0.0 573.9 jit_solution(4957867999160425157)
XLA Ops:
  6.5 0.0 copy-start
  6.5 1.4 dynamic-slice
  8.6 0.9 dynamic-update-slice
  9.5 19.0 %all-reduce = s32[128]{0:T(128)S(1)} all-reduce(s32[128]{0:T(128)S(1)} %dynamic-update-slice), channel_id=1, replica_groups=mesh['dp'=32,'tensor'=8] {'dp'}, use_global_device_ids=true, to_apply=%add | all-reduce | flops 128 | bytes 1024
  28.5 4.8 copy.12
  33.3 0.0 copy-start.2
  33.3 5.8 %reshape.26 = bf16[16,65536]{1,0:T(8,128)(2,1)} reshape(bf16[16,1024,64]{2,1,0:T(8,128)(2,1)} %copy.12) | data formatting | bytes 4194304 | tf_op jit(solution)/shard_map/reshape | solution.py:42
  39.0 0.0 copy-done.2
  39.0 0.2 copy.25
  39.2 0.0 copy-done.3
  39.2 0.2 select_reduce_fusion
  39.4 10.7 %fusion = bf16[128,73728]{1,0:T(8,128)(2,1)} fusion(bf16[16,8192]{1,0:T(8,128)(2,1)S(1)} %bitcast.25, bf16[16,65536]{1,0:T(8,128)(2,1)} %reshape.26, s32[128]{0:T(128)S(1)} %broadcast_subtract_fusion), kind=kOutput, calls=%fused_computation | convolution fusion | flops 306710528 | bytes 21234176 | tf_op jit(solution)/shard_map/dot_general | solution.py:47
  50.1 21.1 %reshape.28 = bf16[32,4,73728]{2,1,0:T(4,128)(2,1)} reshape(bf16[128,73728]{1,0:T(8,128)(2,1)} %fusion) | data formatting | bytes 37748736 | tf_op jit(solution)/shard_map/reshape | solution.py:48
  71.2 8.3 %all-to-all-start = ((bf16[32,4,73728]{2,1,0:T(4,128)(2,1)}), bf16[32,4,73728]{2,1,0:T(4,128)(2,1)}, u32[]{:S(2)}, u32[]{:S(2)}) async-start(bf16[32,4,73728]{2,1,0:T(4,128)(2,1)} %reshape.28), calls=%async_computation.1 | async-start | bytes 37748736 | tf_op jit(solution)/shard_map/all_to_all | solution.py:50
  79.5 0.0 reduce-scatter.2.cloned.1.call-start
  79.6 0.0 copy-done
  79.6 8.9 %fusion.10 = f32[1024,2048]{1,0:T(8,128)} fusion(bf16[1024,1024]{1,0:T(8,128)(2,1)S(1)} %copy-done, bf16[2048,1024]{1,0:T(8,128)(2,1)} %param.6), kind=kOutput, calls=%fused_computation.19 | convolution fusion | flops 4294967296 | bytes 14680064 | tf_op jit(solution)/shard_map/dot_general | solution.py:26
  88.5 0.0 reduce-scatter.2.cloned.1.call-update
  88.6 423.3 %all-to-all-done = bf16[32,4,73728]{2,1,0:T(4,128)(2,1)} async-done(((bf16[32,4,73728]{2,1,0:T(4,128)(2,1)}), bf16[32,4,73728]{2,1,0:T(4,128)(2,1)}, u32[]{:S(2)}, u32[]{:S(2)}) %all-to-all-start) | async-done | bytes 18874400 | tf_op jit(solution)/shard_map/all_to_all | solution.py:50
  511.9 9.3 %reduce_sum.22 = bf16[4,73728]{1,0:T(4,128)(2,1)S(1)} reduce(bf16[32,4,73728]{2,1,0:T(4,128)(2,1)} %all-to-all-done, bf16[]{:T(256)} %constant.14.clone.1), dimensions={0}, to_apply=%region_2.0 | reduce | flops 9142272 | bytes 19464194 | tf_op jit(solution)/shard_map/reduce_sum | solution.py:49
  521.2 0.0 copy-start.1
  521.2 0.8 copy-done.1
  522.0 1.0 slice.8
  523.0 1.9 reshape.29
  524.9 4.4 convolution_bitcast_fusion
  529.3 0.9 slice_bitcast_fusion
  530.2 29.8 %all-reduce.2 = bf16[4,512,64]{1,2,0:T(8,128)(2,1)S(1)} all-reduce(f32[4,512,64]{1,2,0:T(8,128)} %convolution_bitcast_fusion), channel_id=1, replica_groups=mesh['dp'=32,'tensor'=8] {'tensor'}, use_global_device_ids=true, to_apply=%region_3.0 | all-reduce | flops 131072 | bytes 786432 | tf_op jit(solution)/shard_map/psum | solution.py:56
  560.0 1.3 convolution_multiply_fusion
  561.3 1.6 copy.17
  562.9 0.0 reduce-scatter.2.cloned.1.call-done
  562.9 2.1 fusion.4
  565.0 2.0 copy.15
  (3 shorter events, 0.0 us)
Async XLA Ops:
  6.5 73.1 %copy-start = (bf16[1024,1024]{1,0:T(8,128)(2,1)S(1)}, bf16[1024,1024]{1,0:T(8,128)(2,1)}, u32[]{:S(2)}) copy-start(bf16[1024,1024]{1,0:T(8,128)(2,1)} %param.7) | copy-start | bytes 6291460
  33.3 5.8 %copy-start.2 = (bf16[16,64,128]{2,1,0:T(8,128)(2,1)S(1)}, bf16[16,64,128]{2,1,0:T(8,128)(2,1)}, u32[]{:S(2)}) copy-start(bf16[16,64,128]{2,1,0:T(8,128)(2,1)} %param.9) | copy-start | bytes 786436
  33.3 5.9 %copy-start.3 = (s32[512]{0:T(512)S(1)}, s32[512]{0:T(512)}, u32[]{:S(2)}) copy-start(s32[512]{0:T(512)} %param.11) | copy-start | bytes 6148
  71.2 440.7 %all-to-all-start = ((bf16[32,4,73728]{2,1,0:T(4,128)(2,1)}), bf16[32,4,73728]{2,1,0:T(4,128)(2,1)}, u32[]{:S(2)}, u32[]{:S(2)}) async-start(bf16[32,4,73728]{2,1,0:T(4,128)(2,1)} %reshape.28), calls=%async_computation.1 | async-start | bytes 37748736 | tf_op jit(solution)/shard_map/all_to_all | solution.py:50
  79.5 483.3 %reduce-scatter.2.cloned.1.call-start = ((), (), s32[]{:S(2)}) async-start(), calls=%async_computation.2 | async-start | bytes 9437184 | tf_op jit(solution)/shard_map/reduce_scatter | solution.py:25
  521.2 0.8 copy-start.1
Sparse Core Ops, SparseCore 0:
  88.7 56.3 reduce-scatter.1
where the time goes:
time: 575 us; the launch traced here: 574 us
  waiting for transfers between devices  423 us (74%)
  blocking collectives  48.8 us (8%)
  local copies, waits for them, and re-layouts  42.2 us (7%)
  matrix products  25.4 us (4%)
  between operations  14.2 us (2%)
  other arithmetic  11.6 us (2%)
  starting transfers between devices  8.39 us (1%)
    all_to_all x1, waiting for transfers between devices, shards(): lax.all_to_all(outgoing, 'dp', split_axis=0, concat_axis=0, tiled=True)  423 us
    psum x1, blocking collectives, shards(): low = lax.psum(low_part, 'tensor').astype(jnp.bfloat16)  29.8 us
    reshape x1, local copies, waits for them, and re-layouts, shards(): outgoing.reshape(lax.axis_size('dp'), requests_here, panels.shape[1])  21.1 us
    unnamed x1, blocking collectives  19 us
  transfers between devices with their start and end apart: 2, of which 1 were waited for; matrix products, arithmetic and copies ran while one was open for 5% of the time, Pallas kernels for 0%

commit v1 on v0

--- a/solution.py
+++ b/solution.py
@@ -53,7 +53,7 @@
     up_sel = fetched[:, down_width:].reshape(requests_here, adapter_rank_size, local_columns)
     grouped = tokens.reshape(requests_here, seq_len, width)
     low_part = jnp.einsum("rsd,rdk->rsk", grouped, down_sel, preferred_element_type=jnp.float32)
-    low = lax.psum(low_part, "tensor").astype(jnp.bfloat16)
+    low = jnp.sum(lax.all_gather(low_part, "tensor"), axis=0).astype(jnp.bfloat16)
     adapter_update = jnp.einsum("rsk,rkc->rsc", low, up_sel, preferred_element_type=jnp.float32)
     adapter_update = adapter_update.reshape(n_rows, local_columns)
     return (base_projection + adapter_scale * adapter_update).astype(jnp.bfloat16)

time: 575 us -> 606 us (1.054)
  blocking collectives: 48.8 us -> 431 us
  waiting for transfers between devices: 423 us -> 76.5 us
  starting transfers between devices: 8.39 us -> 0.22 us
    all_to_all x1 -> x0, waiting for transfers between devices: 423 us -> none  [shards(): lax.all_to_all(outgoing, 'dp', split_axis=0, concat_axis=0, tiled=True)]
    all_to_all x0 -> x1, blocking collectives: none -> 412 us  [shards(): lax.all_to_all(outgoing, 'dp', split_axis=0, concat_axis=0, tiled=True)]
    reduce_scatter x1, waiting for transfers between devices: 0.02 us -> 51.9 us  [shards(): lax.psum_scatter(lax.dot_general(base_value_weight, tokens, (((0,), (1,))...]
    psum x1 -> x0, blocking collectives: 29.8 us -> none  [shards(): low = lax.psum(low_part, 'tensor').astype(jnp.bfloat16)]
    all_gather x0 -> x1, waiting for transfers between devices: none -> 24.6 us  [shards(): lax.all_gather(low_part, 'tensor')]
    all_to_all x1 -> x0, starting transfers between devices: 8.34 us -> none  [shards(): lax.all_to_all(outgoing, 'dp', split_axis=0, concat_axis=0, tiled=True)]
  transfers between devices with their start and end apart: 2 -> 2, of which waited for: 1 -> 2; matrix products, arithmetic and copies ran while one was open for 5% -> 3% of each run, Pallas kernels for 0% -> 0%
where the time goes in v1:
time: 606 us; the launch traced here: 603 us
  blocking collectives  431 us (71%)
  waiting for transfers between devices  76.5 us (13%)
  local copies, waits for them, and re-layouts  42.1 us (7%)
  matrix products  25.5 us (4%)
  other arithmetic  14.3 us (2%)
  between operations  14.1 us (2%)
    all_to_all x1, blocking collectives, shards(): lax.all_to_all(outgoing, 'dp', split_axis=0, concat_axis=0, tiled=True)  412 us
    reduce_scatter x1, waiting for transfers between devices, shards(): lax.psum_scatter(lax.dot_general(base_value_weight, tokens, (((0,), (1,))...  51.9 us
    all_gather x1, waiting for transfers between devices, shards(): lax.all_gather(low_part, 'tensor')  24.6 us
    reshape x1, local copies, waits for them, and re-layouts, shards(): outgoing.reshape(lax.axis_size('dp'), requests_here, panels.shape[1])  21 us
    unnamed x1, blocking collectives  19 us
  transfers between devices with their start and end apart: 2, of which 2 were waited for; matrix products, arithmetic and copies ran while one was open for 3% of the time, Pallas kernels for 0%

profile of v1, /device:TPU:102, one launch (start us, length us, event | category | flops | bytes accessed | tf_op | source)
XLA Modules:
  0.0 603.5 jit_solution(4029210360239520753)
XLA Ops:
  6.5 0.0 copy-start
  6.5 0.0 all-gather.3.cloned.1.call-start
  6.5 1.4 dynamic-slice
  8.6 0.9 dynamic-update-slice
  9.5 19.0 %all-reduce = s32[128]{0:T(128)S(1)} all-reduce(s32[128]{0:T(128)S(1)} %dynamic-update-slice), channel_id=1, replica_groups=mesh['dp'=32,'tensor'=8] {'dp'}, use_global_device_ids=true, to_apply=%add | all-reduce | flops 128 | bytes 1024
  28.5 4.8 copy.17
  33.3 5.7 reshape.26
  39.0 0.0 copy-done.2
  39.0 0.2 copy.30
  39.2 0.2 select_reduce_fusion
  39.4 10.7 %fusion = bf16[128,73728]{1,0:T(8,128)(2,1)} fusion(bf16[16,8192]{1,0:T(8,128)(2,1)S(1)} %bitcast.27, bf16[16,65536]{1,0:T(8,128)(2,1)} %reshape.26, s32[128]{0:T(128)S(1)} %broadcast_subtract_fusion), kind=kOutput, calls=%fused_computation | convolution fusion | flops 306710528 | bytes 21234176 | tf_op jit(solution)/shard_map/dot_general | solution.py:47
  50.1 21.0 %reshape.28 = bf16[32,4,73728]{2,1,0:T(4,128)(2,1)} reshape(bf16[128,73728]{1,0:T(8,128)(2,1)} %fusion) | data formatting | bytes 37748736 | tf_op jit(solution)/shard_map/reshape | solution.py:48
  71.1 411.6 %all_to_all.5 = bf16[32,4,73728]{2,1,0:T(4,128)(2,1)} all-to-all(bf16[32,4,73728]{2,1,0:T(4,128)(2,1)} %reshape.28), channel_id=1, replica_groups=mesh['dp'=32,'tensor'=8] {'dp'}, dimensions={0} | all-to-all | bytes 37748736 | tf_op jit(solution)/shard_map/all_to_all | solution.py:50
  482.8 9.3 %reduce_sum.31 = bf16[4,73728]{1,0:T(4,128)(2,1)S(1)} reduce(bf16[32,4,73728]{2,1,0:T(4,128)(2,1)} %all_to_all.5, bf16[]{:T(256)} %constant.14.clone.1), dimensions={0}, to_apply=%region_2.0 | reduce | flops 9142272 | bytes 19464194 | tf_op jit(solution)/shard_map/reduce_sum | solution.py:49
  492.1 0.0 copy-start.1
  492.1 0.8 copy-done.1
  492.9 1.0 slice.8
  493.9 1.9 reshape.29
  495.8 4.4 convolution_bitcast_fusion
  500.2 0.0 all-gather.3.cloned.1.call-update
  500.2 0.2 reduce-scatter.2.cloned.1.call-start
  500.4 0.0 copy-done
  500.4 9.0 %fusion.10 = f32[1024,2048]{1,0:T(8,128)} fusion(bf16[1024,1024]{1,0:T(8,128)(2,1)S(1)} %copy-done, bf16[2048,1024]{1,0:T(8,128)(2,1)} %param.6), kind=kOutput, calls=%fused_computation.19 | convolution fusion | flops 4294967296 | bytes 14680064 | tf_op jit(solution)/shard_map/dot_general | solution.py:26
  509.4 0.0 reduce-scatter.2.cloned.1.call-update
  509.5 0.9 slice_bitcast_fusion
  510.3 24.6 %all-gather.3.cloned.1.call-done = f32[32,512,64]{1,2,0:T(8,128)} async-done(((f32[4,512,64]{1,2,0:T(8,128)}), f32[32,512,64]{1,2,0:T(8,128)}) %all-gather.3.cloned.1.call-update) | async-done | bytes 4194320 | tf_op jit(solution)/shard_map/all_gather | solution.py:56
  534.9 2.7 reduce_sum.32
  537.6 1.4 convolution_multiply_fusion
  539.0 1.6 copy.22
  540.6 51.9 %reduce-scatter.2.cloned.1.call-done = f32[128,2048]{1,0:T(8,128)} async-done(((f32[1024,2048]{1,0:T(8,128)}), f32[128,2048]{1,0:T(8,128)}) %reduce-scatter.2.cloned.1.call-update) | async-done | bytes 1048592 | tf_op jit(solution)/shard_map/reduce_scatter | solution.py:25
  592.5 2.1 fusion.4
  594.6 2.0 copy.20
  (5 shorter events, 0.0 us)
Async XLA Ops:
  6.5 493.9 %copy-start = (bf16[1024,1024]{1,0:T(8,128)(2,1)S(1)}, bf16[1024,1024]{1,0:T(8,128)(2,1)}, u32[]{:S(2)}) copy-start(bf16[1024,1024]{1,0:T(8,128)(2,1)} %param.7) | copy-start | bytes 6291460
  6.5 528.4 %all-gather.3.cloned.1.call-start = ((), (), s32[]{:S(2)}) async-start(), calls=%async_computation.3 | async-start | bytes 4718592 | tf_op jit(solution)/shard_map/all_gather | solution.py:56
  33.3 5.7 copy-start.2
  33.3 5.9 copy-start.3
  492.1 0.8 copy-start.1
  500.2 92.3 %reduce-scatter.2.cloned.1.call-start = ((), (), s32[]{:S(2)}) async-start(), calls=%async_computation.2 | async-start | bytes 9437184 | tf_op jit(solution)/shard_map/reduce_scatter | solution.py:25
Sparse Core Ops, SparseCore 0:
  500.3 34.5 all-gather.2
  537.5 54.9 reduce-scatter.1
